TPU v7x, 32 devices: a whole 2x2x4 slice. The times are simulated.
32 devices in a mesh: beam: 2 (over x), rng: 16 (over z, y, core).
Axes of the slice: x: 2, y: 2, z: 4, core: 2. Of those that a mesh axis runs over, the one named last changes fastest.
Arguments:
- echoes: bfloat16 [4, 1024, 8192], P('beam', 'rng'), parts along dimension 0, may hold values from -6 to 6
- phase_code: int32 [256], replicated, may hold values from -1 to 1, as said below
Outputs:
- test_ratio: float32 [2048, 8192], P('beam', 'rng'), parts along dimension 0
There are 2 independent parts, one for each index of `beam`. A program takes and returns all parts, laid end to end along the dimension named above; an argument that names none is the same for every part. Nothing has to cross between parts.
Inputs may be any that keep to these rules, and one draw needn't show every extreme that they name: `phase_code`: each entry is -1 or +1.
All inputs are finite; a program needn't handle non-finite values.
Results may differ from a plain program's by a relative error of at most 0.0039.
Values may be sent and summed in bfloat16 or wider, within the bound.
A program may use at most 128 MiB of HBM per device.

v0:
```python
import math
import jax
import jax.numpy as jnp
from jax import lax
from jax.sharding import PartitionSpec as P

WIN_R = 33
WIN_D = 9
GUARD_R = 5
GUARD_D = 3


def extended(cells, sides, width):
    for axis, dim in sides:
        count = lax.axis_size(axis)
        ends = count - 1
        head = lax.slice_in_dim(cells, 0, width, axis=dim)
        tail = lax.slice_in_dim(cells, cells.shape[dim] - width, cells.shape[dim], axis=dim)
        cells = jnp.concatenate(
            [
                lax.ppermute(tail, axis, [(i, (i + 1) % count) for i in range(ends)]),
                cells,
                lax.ppermute(head, axis, [((i + 1) % count, i) for i in range(ends)]),
            ],
            axis=dim,
        )
    return cells


def toeplitz_pair(phase_code):
    length = phase_code.shape[0]
    values = phase_code.astype(jnp.float32)
    padded_code = jnp.concatenate([values, jnp.zeros((length,), jnp.float32)])
    rotated = jnp.roll(padded_code, length - 1)
    repeated = jnp.tile(rotated, length + 1)[: length * (2 * length + 1)]
    rows_made = repeated.reshape(length, 2 * length + 1)[:, : 2 * length]
    return rows_made[::-1].T.astype(jnp.bfloat16)


def compress_rows(echo_rows, next_tail, filter_pair):
    length = filter_pair.shape[1]
    row_count = echo_rows.shape[0]
    cell_count = echo_rows.shape[1]
    blocks = cell_count // length
    upper_half = filter_pair[:length]
    lower_half = filter_pair[length:]
    block_rows = echo_rows.reshape(row_count * blocks, length)
    own_terms = jnp.dot(block_rows, upper_half, preferred_element_type=jnp.float32).reshape(
        row_count, blocks, length
    )
    next_terms = jnp.dot(block_rows, lower_half, preferred_element_type=jnp.float32).reshape(
        row_count, blocks, length
    )
    tail_terms = jnp.dot(next_tail, lower_half, preferred_element_type=jnp.float32).reshape(
        row_count, 1, length
    )
    result = own_terms + jnp.concatenate([next_terms[:, 1:], tail_terms], axis=1)
    return result.reshape(row_count, cell_count).astype(jnp.bfloat16)


def doppler_table(pulses):
    index_all = jnp.arange(pulses, dtype=jnp.int32)
    phase_angle = (index_all[:, None] * index_all[None, :] % pulses).astype(jnp.float32) * (
        2.0 * math.pi / pulses
    )
    window_taper = 0.5 - 0.5 * jnp.cos(
        (index_all.astype(jnp.float32) + 0.5) * (2.0 * math.pi / pulses)
    )
    cosine = window_taper[None, :] * jnp.cos(phase_angle)
    sine_part = window_taper[None, :] * jnp.sin(phase_angle)
    top_rows = jnp.concatenate([cosine, sine_part], axis=1)
    bottom_rows = jnp.concatenate([-sine_part, cosine], axis=1)
    return jnp.concatenate([top_rows, bottom_rows], axis=0).astype(jnp.bfloat16)


def power_of(table, compressed):
    pulses = compressed.shape[1]
    stacked = compressed.reshape(2 * pulses, compressed.shape[2])
    spectrum = jnp.dot(table, stacked, preferred_element_type=jnp.float32)
    return spectrum[:pulses] * spectrum[:pulses] + spectrum[pulses:] * spectrum[pulses:]


def range_sums(padded, half_width, margin):
    cell_count = padded.shape[-1] - 2 * margin
    running = padded[..., margin - half_width : margin - half_width + cell_count]
    for offset in range(margin - half_width + 1, margin + half_width + 1):
        running = running + padded[..., offset : offset + cell_count]
    return running


def slice_sums(wrapped, half_width, reach, pulses):
    running = wrapped[reach - half_width : reach - half_width + pulses]
    for offset in range(reach - half_width + 1, reach + half_width + 1):
        running = running + wrapped[offset : offset + pulses]
    return running


def cfar_ratio(padded, valid_mask):
    margin = WIN_R // 2
    reach = WIN_D // 2
    pulses = padded.shape[0]
    wrapped = jnp.concatenate([padded[pulses - reach :], padded, padded[:reach]], axis=0)
    wide_sums = range_sums(wrapped, WIN_R // 2, margin)
    guard_sums = range_sums(wrapped, GUARD_R // 2, margin)
    train_sums = slice_sums(wide_sums, WIN_D // 2, reach, pulses) - slice_sums(
        guard_sums, GUARD_D // 2, reach, pulses
    )
    train_count = (
        range_sums(valid_mask, WIN_R // 2, margin) * WIN_D
        - range_sums(valid_mask, GUARD_R // 2, margin) * GUARD_D
    )
    noise_level = train_sums / train_count[None, :]
    center_power = padded[:, margin : padded.shape[1] - margin]
    return center_power / noise_level


def corner_turn(signal):
    return lax.all_to_all(signal, "rng", split_axis=2, concat_axis=1, tiled=True)


def local(echoes, phase_code):
    filter_pair = toeplitz_pair(phase_code)
    length = phase_code.shape[0]
    local_pulses = echoes.shape[1]
    all_cells = echoes.shape[2]
    local_rows = echoes.reshape(2 * local_pulses, all_cells)
    zero_tail = jnp.zeros((2 * local_pulses, length), jnp.bfloat16)
    local_compressed = compress_rows(local_rows, zero_tail, filter_pair).reshape(
        2, local_pulses, all_cells
    )
    compressed = corner_turn(local_compressed)
    pulses = compressed.shape[1]
    cell_count = compressed.shape[2]
    table = doppler_table(pulses)
    margin = WIN_R // 2
    power_map = power_of(table, compressed)
    padded = extended(power_map, (("rng", 1),), margin)
    position = (
        lax.axis_index("rng") * cell_count
        + jnp.arange(cell_count + 2 * margin, dtype=jnp.int32)
        - margin
    )
    total_cells = cell_count * lax.axis_size("rng")
    valid_mask = ((position >= 0) & (position < total_cells)).astype(jnp.float32)
    return cfar_ratio(padded, valid_mask)


def solution(mesh):
    placed = (P("beam", "rng", None), P())
    return jax.shard_map(
        local, mesh=mesh, in_specs=placed, out_specs=P("beam", "rng"), check_vma=False
    )
```

profile of v0, /device:TPU:13, one launch (start us, length us, event | category | flops | bytes accessed | tf_op | source)
XLA Modules:
  0.0 180.7 jit_solution(8680494630458086528)
XLA Ops:
  0.0 0.7 convert_element_type.41
  1.0 0.6 reshape.33
  1.6 0.3 rev.3
  1.9 2.9 %reshape_reshape.3 = bf16[4096,256]{1,0:T(8,128)(2,1)S(1)} reshape(bf16[2,64,8192]{2,1,0:T(8,128)(2,1)} %param.2) | data formatting | bytes 4194304 | tf_op jit(solution)/shard_map/reshape;reshape | solution.py:47
  5.0 2.7 %convolution_bitcast_fusion = f32[4096,256]{0,1:T(8,128)} fusion(bf16[4096,256]{1,0:T(8,128)(2,1)S(1)} %reshape_reshape.3, bf16[512,256]{0,1:T(8,128)(2,1)S(1)} %bitcast.26), kind=kOutput, calls=%fused_computation.11 | convolution fusion | flops 536870912 | bytes 6422528 | tf_op jit(solution)/shard_map/dot_general | solution.py:51
  7.7 2.7 %convolution_bitcast_fusion.1 = f32[4096,256]{0,1:T(8,128)} fusion(bf16[4096,256]{1,0:T(8,128)(2,1)S(1)} %reshape_reshape.3, bf16[512,256]{0,1:T(8,128)(2,1)S(1)} %bitcast.27), kind=kOutput, calls=%fused_computation.12 | convolution fusion | flops 536870912 | bytes 6422528 | tf_op jit(solution)/shard_map/dot_general | solution.py:48
  10.4 5.6 %copy.16 = f32[4096,256]{1,0:T(8,128)} copy(f32[4096,256]{0,1:T(8,128)} %convolution_bitcast_fusion) | data formatting | bytes 8388608 | tf_op jit(solution)/shard_map/dot_general | solution.py:51
  16.0 2.8 %slice.379 = f32[128,31,256]{2,1,0:T(8,128)S(1)} slice(f32[128,32,256]{2,1,0:T(8,128)} %bitcast.23), slice={[0:128], [1:32], [0:256]} | slice | bytes 8126464 | tf_op jit(solution)/shard_map/slice | solution.py:57
  18.9 2.5 %pad_maximum_fusion = f32[128,32,256]{2,1,0:T(8,128)} fusion(f32[128,1,256]{2,1,0:T(1,128)S(1)} %copy.17, f32[128,31,256]{2,1,0:T(8,128)S(1)} %slice.379), kind=kLoop, calls=%fused_computation.16 | loop fusion | flops 1048576 | bytes 8388608 | tf_op jit(solution)/shard_map/concatenate | solution.py:57
  21.5 5.0 %concatenate.36 = f32[2,64,8192]{2,1,0:T(8,128)} reshape(f32[128,32,256]{2,1,0:T(8,128)} %pad_maximum_fusion) | data formatting | bytes 8388608 | tf_op jit(solution)/shard_map/concatenate | solution.py:57
  26.4 5.6 %copy.15 = f32[4096,256]{1,0:T(8,128)} copy(f32[4096,256]{0,1:T(8,128)} %convolution_bitcast_fusion.1) | data formatting | bytes 8388608 | tf_op jit(solution)/shard_map/dot_general | solution.py:48
  32.1 4.9 %reshape.34 = f32[2,64,8192]{2,1,0:T(8,128)} reshape(f32[4096,256]{1,0:T(8,128)} %copy.15) | data formatting | bytes 8388608 | tf_op jit(solution)/shard_map/reshape | solution.py:48
  37.0 3.9 %add_convert_fusion = bf16[2,64,8192]{2,1,0:T(8,128)(2,1)S(1)} fusion(f32[2,64,8192]{2,1,0:T(8,128)} %reshape.34, f32[2,64,8192]{2,1,0:T(8,128)} %concatenate.36), kind=kLoop, calls=%fused_computation.17 | loop fusion | flops 2097152 | bytes 10485760 | tf_op jit(solution)/shard_map/convert_element_type | solution.py:58
  40.9 6.9 %copy.18 = bf16[2,64,8192]{1,0,2:T(2,128)(2,1)} copy(bf16[2,64,8192]{2,1,0:T(8,128)(2,1)S(1)} %add_convert_fusion) | data formatting | bytes 4194304 | tf_op jit(solution)/shard_map/convert_element_type | solution.py:58
  47.8 7.5 %reshape.38 = bf16[16,2,32768]{2,1,0:T(2,128)(2,1)} reshape(bf16[8192,2,64]{2,1,0:T(2,128)(2,1)} %bitcast.21) | data formatting | bytes 4194304
  55.3 6.6 %all-to-all-start = ((bf16[16,2,32768]{2,1,0:T(2,128)(2,1)}), bf16[16,2,32768]{2,1,0:T(2,128)(2,1)S(1)}, u32[]{:S(2)}, u32[]{:S(2)}) async-start(bf16[16,2,32768]{2,1,0:T(2,128)(2,1)} %reshape.38), calls=%async_computation | async-start | bytes 4194304 | tf_op jit(solution)/shard_map/all_to_all | solution.py:118
  61.9 19.0 %fusion.14 = (bf16[1024,1024]{1,0:T(8,128)(2,1)}, bf16[1024,1024]{1,0:T(8,128)(2,1)}, bf16[1024,1024]{1,0:T(8,128)(2,1)}) fusion(f32[1024]{0:T(1024)S(1)} %multiply_subtract_fusion), kind=kLoop, calls=%fused_computation.24 | loop fusion | flops 20971520 | bytes 6295552 | tf_op jit(solution)/shard_map/convert.5
  80.9 28.3 %all-to-all-done = bf16[16,2,32768]{2,1,0:T(2,128)(2,1)S(1)} async-done(((bf16[16,2,32768]{2,1,0:T(2,128)(2,1)}), bf16[16,2,32768]{2,1,0:T(2,128)(2,1)S(1)}, u32[]{:S(2)}, u32[]{:S(2)}) %all-to-all-start) | async-done | bytes 2097184 | tf_op jit(solution)/shard_map/all_to_all | solution.py:118
  109.3 5.0 %reshape.39 = bf16[8192,2,64]{2,1,0:T(2,128)(2,1)} reshape(bf16[16,2,32768]{2,1,0:T(2,128)(2,1)S(1)} %all-to-all-done) | data formatting | bytes 4194304
  114.2 9.1 %copy.23 = bf16[2,64,16,512]{3,1,2,0:T(8,128)(2,1)S(1)} copy(bf16[2,64,16,512]{1,0,3,2:T(2,128)(2,1)} %bitcast.22) | data formatting | bytes 4194304 | tf_op jit(solution)/shard_map/all_to_all | solution.py:118
  123.3 10.6 %fusion = f32[2048,512]{0,1:T(8,128)S(1)} fusion(bf16[2048,512]{1,0:T(8,128)(2,1)S(1)} %bitcast.24, bf16[1024,1024]{1,0:T(8,128)(2,1)} %get-tuple-element.11, bf16[1024,1024]{1,0:T(8,128)(2,1)} %get-tuple-element.10, bf16[1024,1024]{1,0:T(8,128)(2,1)} %get-tuple-element.9), kind=kOutput, calls=%fused_computation | convolution fusion | flops 4328521728 | bytes 12582912 | tf_op jit(solution)/shard_map/dot_general | solution.py:79
  133.9 0.4 fusion.22
  134.4 1.5 copy-done
  135.8 3.6 %collective-permute-start = (f32[1024,16]{0,1:T(8,128)S(1)}, f32[1024,16]{0,1:T(8,128)S(1)}, u32[]{:S(2)}, u32[]{:S(2)}) collective-permute-start(f32[1024,16]{0,1:T(8,128)S(1)} %get-tuple-element.7), channel_id=1, source_target_pairs={{0,1},{1,2},{2,3},{3,4},{4,5},{5,6},{6,7},{7,8},{8,9},{9,10},{10,1... | collective-permute-start | bytes 196616 | tf_op jit(solution)/shard_map/ppermute | solution.py:21
  139.4 2.1 %collective-permute-start.1 = (f32[1024,16]{0,1:T(8,128)S(1)}, f32[1024,16]{0,1:T(8,128)S(1)}, u32[]{:S(2)}, u32[]{:S(2)}) collective-permute-start(f32[1024,16]{0,1:T(8,128)S(1)} %get-tuple-element.8), channel_id=1, source_target_pairs={{1,0},{2,1},{3,2},{4,3},{5,4},{6,5},{7,6},{8,7},{9,8},{10,9},{11,1... | collective-permute-start | bytes 196616 | tf_op jit(solution)/shard_map/ppermute | solution.py:23
  141.7 4.2 %collective-permute-done.1 = f32[1024,16]{0,1:T(8,128)S(1)} collective-permute-done((f32[1024,16]{0,1:T(8,128)S(1)}, f32[1024,16]{0,1:T(8,128)S(1)}, u32[]{:S(2)}, u32[]{:S(2)}) %collective-permute-start.1) | collective-permute-done | bytes 65568 | tf_op jit(solution)/shard_map/ppermute | solution.py:23
  146.3 1.2 copy-done.1
  147.6 3.2 %concatenate.38 = f32[1032,544]{0,1:T(8,128)S(1)} concatenate(f32[4,544]{0,1:T(8,128)S(1)} %get-tuple-element.6, f32[1024,544]{0,1:T(8,128)} %copy-done.1, f32[4,544]{0,1:T(8,128)S(1)} %get-tuple-element.5), dimensions={0} | concatenate | bytes 4491264 | tf_op jit(solution)/shard_map/concatenate | solution.py:102
  150.7 2.3 %add_add_fusion = f32[1032,512]{0,1:T(8,128)} fusion(f32[1032,544]{0,1:T(8,128)S(1)} %concatenate.38), kind=kLoop, calls=%fused_computation.57 | loop fusion | flops 2113536 | bytes 12681216 | tf_op jit(solution)/shard_map/add | solution.py:87
  153.1 7.7 %slice_add_fusion = f32[1032,512]{0,1:T(8,128)} fusion(f32[1032,544]{0,1:T(8,128)S(1)} %concatenate.38), kind=kLoop, calls=%fused_computation.25 | loop fusion | flops 16908288 | bytes 71860224 | tf_op jit(solution)/shard_map/add | solution.py:87
  160.8 18.1 %fusion.21 = f32[1024,512]{0,1:T(8,128)S(1)} fusion(f32[1032,512]{0,1:T(8,128)} %add_add_fusion, f32[1032,512]{0,1:T(8,128)} %slice_add_fusion, f32[512]{0:T(512)S(1)} %multiply_subtract_fusion.1, f32[2048,512]{0,1:T(8,128)} %copy-done), kind=kLoop, calls=%fused_computation.61 | loop fusion | flops 8388608 | bytes 31459328 | tf_op jit(solution)/shard_map/div | solution.py:114
  178.8 1.8 %copy.21 = f32[1024,512]{1,0:T(8,128)} copy(f32[1024,512]{0,1:T(8,128)S(1)} %fusion.21) | data formatting | bytes 4194304 | tf_op jit(solution)/shard_map/div | solution.py:114
  (16 shorter events, 1.2 us)
Async XLA Ops:
  55.3 54.0 %all-to-all-start = ((bf16[16,2,32768]{2,1,0:T(2,128)(2,1)}), bf16[16,2,32768]{2,1,0:T(2,128)(2,1)S(1)}, u32[]{:S(2)}, u32[]{:S(2)}) async-start(bf16[16,2,32768]{2,1,0:T(2,128)(2,1)} %reshape.38), calls=%async_computation | async-start | bytes 4194304 | tf_op jit(solution)/shard_map/all_to_all | solution.py:118
  133.9 1.9 %copy-start = (f32[2048,512]{0,1:T(8,128)}, f32[2048,512]{0,1:T(8,128)S(1)}, u32[]{:S(2)}) copy-start(f32[2048,512]{0,1:T(8,128)S(1)} %fusion) | copy-start | bytes 12582916
  135.8 5.8 %collective-permute-start = (f32[1024,16]{0,1:T(8,128)S(1)}, f32[1024,16]{0,1:T(8,128)S(1)}, u32[]{:S(2)}, u32[]{:S(2)}) collective-permute-start(f32[1024,16]{0,1:T(8,128)S(1)} %get-tuple-element.7), channel_id=1, source_target_pairs={{0,1},{1,2},{2,3},{3,4},{4,5},{5,6},{6,7},{7,8},{8,9},{9,10},{10,1... | collective-permute-start | bytes 196616 | tf_op jit(solution)/shard_map/ppermute | solution.py:21
  139.4 6.5 %collective-permute-start.1 = (f32[1024,16]{0,1:T(8,128)S(1)}, f32[1024,16]{0,1:T(8,128)S(1)}, u32[]{:S(2)}, u32[]{:S(2)}) collective-permute-start(f32[1024,16]{0,1:T(8,128)S(1)} %get-tuple-element.8), channel_id=1, source_target_pairs={{1,0},{2,1},{3,2},{4,3},{5,4},{6,5},{7,6},{8,7},{9,8},{10,9},{11,1... | collective-permute-start | bytes 196616 | tf_op jit(solution)/shard_map/ppermute | solution.py:23
  146.2 1.4 copy-start.1
where the time goes:
time: 182 us; the launch traced here: 181 us
  local copies, waits for them, and re-layouts  64.4 us (35%)
  other arithmetic  55.1 us (30%)
  waiting for transfers between devices  32.5 us (18%)
  matrix products  16.1 us (9%)
  starting transfers between devices  12.3 us (7%)
    all_to_all x1, waiting for transfers between devices, corner_turn(): lax.all_to_all(signal, 'rng', split_axis=2, concat_axis=1, tiled=True)  28.3 us
    another operation x1, other arithmetic  19 us
    div x1, other arithmetic, cfar_ratio(): return center_power / noise_level  18.1 us
    unnamed x6, local copies, waits for them, and re-layouts  15.2 us
    dot_general x1, matrix products, power_of(): spectrum = jnp.dot(table, stacked, preferred_element_type=jnp.float32)  10.6 us
    add x2, other arithmetic, range_sums(): running = running + padded[..., offset:offset + cell_count]  10 us
    all_to_all x1, local copies, waits for them, and re-layouts, corner_turn(): lax.all_to_all(signal, 'rng', split_axis=2, concat_axis=1, tiled=True)  9.07 us
    convert_element_type x1, local copies, waits for them, and re-layouts, compress_rows(): return result.reshape(row_count, cell_count).astype(jnp.bfloat16)  6.89 us
  transfers between devices with their start and end apart: 3, of which 2 were waited for; matrix products, arithmetic and copies ran while one was open for 11% of the time, Pallas kernels for 0%

commit v1 on v0

--- a/solution.py
+++ b/solution.py
@@ -115,7 +115,10 @@
 
 
 def corner_turn(signal):
-    return lax.all_to_all(signal, "rng", split_axis=2, concat_axis=1, tiled=True)
+    return jnp.concatenate(
+        lax.all_to_all(jnp.stack(jnp.split(signal, lax.axis_size("rng"), axis=2)), "rng", 0, 0),
+        axis=1,
+    )
 
 
 def local(echoes, phase_code):

time: 182 us -> 164 us (0.901)
  local copies, waits for them, and re-layouts: 64.4 us -> 46.7 us
    all_to_all x1 -> x0, local copies, waits for them, and re-layouts: 9.07 us -> none  [corner_turn(): lax.all_to_all(signal, 'rng', split_axis=2, concat_axis=1, tiled=True)]
    convert_element_type x1 -> x0, local copies, waits for them, and re-layouts: 6.89 us -> none  [compress_rows(): return result.reshape(row_count, cell_count).astype(jnp.bfloat16)]
    unnamed x6 -> x19, local copies, waits for them, and re-layouts: 15.2 us -> 12.7 us
  transfers between devices with their start and end apart: 3 -> 3, of which waited for: 2 -> 2; matrix products, arithmetic and copies ran while one was open for 11% -> 12% of each run, Pallas kernels for 0% -> 0%
where the time goes in v1:
time: 164 us; the launch traced here: 163 us
  other arithmetic  55.1 us (34%)
  local copies, waits for them, and re-layouts  46.7 us (28%)
  waiting for transfers between devices  32.5 us (20%)
  matrix products  16.3 us (10%)
  starting transfers between devices  12.3 us (8%)
    all_to_all x1, waiting for transfers between devices, corner_turn(): lax.all_to_all(jnp.stack(jnp.split(signal, lax.axis_size('rng'), axis=2))...  28.3 us
    another operation x1, other arithmetic  19 us
    div x1, other arithmetic, cfar_ratio(): return center_power / noise_level  18.1 us
    unnamed x19, local copies, waits for them, and re-layouts  12.7 us
    dot_general x1, matrix products, power_of(): spectrum = jnp.dot(table, stacked, preferred_element_type=jnp.float32)  10.7 us
    add x2, other arithmetic, range_sums(): running = running + padded[..., offset:offset + cell_count]  10 us
    all_to_all x1, starting transfers between devices, corner_turn(): lax.all_to_all(jnp.stack(jnp.split(signal, lax.axis_size('rng'), axis=2))...  6.56 us
    dot_general x1, local copies, waits for them, and re-layouts, compress_rows(): jnp.dot(block_rows, lower_half, preferred_element_type=jnp.float32)  5.61 us
  transfers between devices with their start and end apart: 3, of which 2 were waited for; matrix products, arithmetic and copies ran while one was open for 12% of the time, Pallas kernels for 0%

profile of v1, /device:TPU:13, one launch (start us, length us, event | category | flops | bytes accessed | tf_op | source)
XLA Modules:
  0.0 163.1 jit_solution(352833490076749083)
XLA Ops:
  0.0 0.7 convert_element_type.41
  1.9 2.9 %reshape_reshape.6 = bf16[4096,256]{1,0:T(8,128)(2,1)S(1)} reshape(bf16[2,64,8192]{2,1,0:T(8,128)(2,1)} %param.2) | data formatting | bytes 4194304 | tf_op jit(solution)/shard_map/reshape;reshape | solution.py:47
  5.0 2.7 %convolution_bitcast_fusion = f32[4096,256]{0,1:T(8,128)} fusion(bf16[4096,256]{1,0:T(8,128)(2,1)S(1)} %reshape_reshape.6, bf16[512,256]{0,1:T(8,128)(2,1)S(1)} %bitcast.84), kind=kOutput, calls=%fused_computation.11 | convolution fusion | flops 536870912 | bytes 6422528 | tf_op jit(solution)/shard_map/dot_general | solution.py:51
  7.7 2.7 %convolution_bitcast_fusion.1 = f32[4096,256]{0,1:T(8,128)} fusion(bf16[4096,256]{1,0:T(8,128)(2,1)S(1)} %reshape_reshape.6, bf16[512,256]{0,1:T(8,128)(2,1)S(1)} %bitcast.85), kind=kOutput, calls=%fused_computation.12 | convolution fusion | flops 536870912 | bytes 6422528 | tf_op jit(solution)/shard_map/dot_general | solution.py:48
  10.4 5.6 %copy.6 = f32[4096,256]{1,0:T(8,128)} copy(f32[4096,256]{0,1:T(8,128)} %convolution_bitcast_fusion) | data formatting | bytes 8388608 | tf_op jit(solution)/shard_map/dot_general | solution.py:51
  16.0 2.8 %slice.379 = f32[128,31,256]{2,1,0:T(8,128)S(1)} slice(f32[128,32,256]{2,1,0:T(8,128)} %bitcast.80), slice={[0:128], [1:32], [0:256]} | slice | bytes 8126464 | tf_op jit(solution)/shard_map/slice | solution.py:57
  18.9 2.5 %pad_maximum_fusion = f32[128,32,256]{2,1,0:T(8,128)} fusion(f32[128,1,256]{2,1,0:T(1,128)S(1)} %copy.7, f32[128,31,256]{2,1,0:T(8,128)S(1)} %slice.379), kind=kLoop, calls=%fused_computation.16 | loop fusion | flops 1048576 | bytes 8388608 | tf_op jit(solution)/shard_map/concatenate | solution.py:57
  21.5 5.0 %concatenate.36 = f32[2,64,8192]{2,1,0:T(8,128)} reshape(f32[128,32,256]{2,1,0:T(8,128)} %pad_maximum_fusion) | data formatting | bytes 8388608 | tf_op jit(solution)/shard_map/concatenate | solution.py:57
  26.4 5.6 %copy.5 = f32[4096,256]{1,0:T(8,128)} copy(f32[4096,256]{0,1:T(8,128)} %convolution_bitcast_fusion.1) | data formatting | bytes 8388608 | tf_op jit(solution)/shard_map/dot_general | solution.py:48
  32.1 4.9 %reshape.33 = f32[2,64,8192]{2,1,0:T(8,128)} reshape(f32[4096,256]{1,0:T(8,128)} %copy.5) | data formatting | bytes 8388608 | tf_op jit(solution)/shard_map/reshape | solution.py:48
  37.0 3.9 %add_convert_fusion = bf16[2,64,8192]{2,1,0:T(8,128)(2,1)S(1)} fusion(f32[2,64,8192]{2,1,0:T(8,128)} %reshape.33, f32[2,64,8192]{2,1,0:T(8,128)} %concatenate.36), kind=kLoop, calls=%fused_computation.17 | loop fusion | flops 2097152 | bytes 10485760 | tf_op jit(solution)/shard_map/convert_element_type | solution.py:58
  40.9 0.7 fusion.38
  41.5 0.7 fusion.37
  42.2 0.7 fusion.36
  42.9 0.7 fusion.35
  43.5 0.7 fusion.34
  44.2 0.7 fusion.33
  50.8 0.7 fusion.23
  51.5 6.6 %all-to-all-start = ((bf16[16,2,64,512]{3,2,1,0:T(8,128)(2,1)}), bf16[16,2,64,512]{3,2,1,0:T(8,128)(2,1)S(1)}, u32[]{:S(2)}, u32[]{:S(2)}) async-start(bf16[16,2,64,512]{3,2,1,0:T(8,128)(2,1)} %fusion.23), calls=%async_computation | async-start | bytes 4194304 | tf_op jit(solution)/shard_map/all_to_all | solution.py:119
  58.1 19.0 %fusion.14 = (bf16[1024,1024]{1,0:T(8,128)(2,1)}, bf16[1024,1024]{1,0:T(8,128)(2,1)}, bf16[1024,1024]{1,0:T(8,128)(2,1)}) fusion(f32[1024]{0:T(1024)S(1)} %multiply_subtract_fusion), kind=kLoop, calls=%fused_computation.24 | loop fusion | flops 20971520 | bytes 6295552 | tf_op jit(solution)/shard_map/convert.5
  77.2 28.3 %all-to-all-done = bf16[16,2,64,512]{3,2,1,0:T(8,128)(2,1)S(1)} async-done(((bf16[16,2,64,512]{3,2,1,0:T(8,128)(2,1)}), bf16[16,2,64,512]{3,2,1,0:T(8,128)(2,1)S(1)}, u32[]{:S(2)}, u32[]{:S(2)}) %all-to-all-start) | async-done | bytes 2097184 | tf_op jit(solution)/shard_map/all_to_all | solution.py:119
  105.6 10.7 %fusion = f32[2048,512]{0,1:T(8,128)S(1)} fusion(bf16[2048,512]{1,0:T(8,128)(2,1)S(1)} %bitcast.82, bf16[1024,1024]{1,0:T(8,128)(2,1)} %get-tuple-element.11, bf16[1024,1024]{1,0:T(8,128)(2,1)} %get-tuple-element.10, bf16[1024,1024]{1,0:T(8,128)(2,1)} %get-tuple-element.9), kind=kOutput, calls=%fused_computation | convolution fusion | flops 4328521728 | bytes 12582912 | tf_op jit(solution)/shard_map/dot_general | solution.py:79
  116.8 1.5 copy-done
  118.3 3.6 %collective-permute-start = (f32[1024,16]{0,1:T(8,128)S(1)}, f32[1024,16]{0,1:T(8,128)S(1)}, u32[]{:S(2)}, u32[]{:S(2)}) collective-permute-start(f32[1024,16]{0,1:T(8,128)S(1)} %get-tuple-element.7), channel_id=1, source_target_pairs={{0,1},{1,2},{2,3},{3,4},{4,5},{5,6},{6,7},{7,8},{8,9},{9,10},{10,1... | collective-permute-start | bytes 196616 | tf_op jit(solution)/shard_map/ppermute | solution.py:21
  121.9 2.1 %collective-permute-start.1 = (f32[1024,16]{0,1:T(8,128)S(1)}, f32[1024,16]{0,1:T(8,128)S(1)}, u32[]{:S(2)}, u32[]{:S(2)}) collective-permute-start(f32[1024,16]{0,1:T(8,128)S(1)} %get-tuple-element.8), channel_id=1, source_target_pairs={{1,0},{2,1},{3,2},{4,3},{5,4},{6,5},{7,6},{8,7},{9,8},{10,9},{11,1... | collective-permute-start | bytes 196616 | tf_op jit(solution)/shard_map/ppermute | solution.py:23
  124.1 4.2 %collective-permute-done.1 = f32[1024,16]{0,1:T(8,128)S(1)} collective-permute-done((f32[1024,16]{0,1:T(8,128)S(1)}, f32[1024,16]{0,1:T(8,128)S(1)}, u32[]{:S(2)}, u32[]{:S(2)}) %collective-permute-start.1) | collective-permute-done | bytes 65568 | tf_op jit(solution)/shard_map/ppermute | solution.py:23
  128.8 1.2 copy-done.1
  130.0 3.2 %concatenate.38 = f32[1032,544]{0,1:T(8,128)S(1)} concatenate(f32[4,544]{0,1:T(8,128)S(1)} %get-tuple-element.6, f32[1024,544]{0,1:T(8,128)} %copy-done.1, f32[4,544]{0,1:T(8,128)S(1)} %get-tuple-element.5), dimensions={0} | concatenate | bytes 4491264 | tf_op jit(solution)/shard_map/concatenate | solution.py:102
  133.2 2.3 %add_add_fusion = f32[1032,512]{0,1:T(8,128)} fusion(f32[1032,544]{0,1:T(8,128)S(1)} %concatenate.38), kind=kLoop, calls=%fused_computation.57 | loop fusion | flops 2113536 | bytes 12681216 | tf_op jit(solution)/shard_map/add | solution.py:87
  135.5 7.7 %slice_add_fusion = f32[1032,512]{0,1:T(8,128)} fusion(f32[1032,544]{0,1:T(8,128)S(1)} %concatenate.38), kind=kLoop, calls=%fused_computation.25 | loop fusion | flops 16908288 | bytes 71860224 | tf_op jit(solution)/shard_map/add | solution.py:87
  143.2 18.1 %fusion.21 = f32[1024,512]{0,1:T(8,128)S(1)} fusion(f32[1032,512]{0,1:T(8,128)} %add_add_fusion, f32[1032,512]{0,1:T(8,128)} %slice_add_fusion, f32[512]{0:T(512)S(1)} %multiply_subtract_fusion.1, f32[2048,512]{0,1:T(8,128)} %copy-done), kind=kLoop, calls=%fused_computation.61 | loop fusion | flops 8388608 | bytes 31459328 | tf_op jit(solution)/shard_map/div | solution.py:114
  161.3 1.8 %copy.9 = f32[1024,512]{1,0:T(8,128)} copy(f32[1024,512]{0,1:T(8,128)S(1)} %fusion.21) | data formatting | bytes 4194304 | tf_op jit(solution)/shard_map/div | solution.py:114
  (29 shorter events, 8.6 us)
Async XLA Ops:
  51.5 54.0 %all-to-all-start = ((bf16[16,2,64,512]{3,2,1,0:T(8,128)(2,1)}), bf16[16,2,64,512]{3,2,1,0:T(8,128)(2,1)S(1)}, u32[]{:S(2)}, u32[]{:S(2)}) async-start(bf16[16,2,64,512]{3,2,1,0:T(8,128)(2,1)} %fusion.23), calls=%async_computation | async-start | bytes 4194304 | tf_op jit(solution)/shard_map/all_to_all | solution.py:119
  116.3 1.9 %copy-start = (f32[2048,512]{0,1:T(8,128)}, f32[2048,512]{0,1:T(8,128)S(1)}, u32[]{:S(2)}) copy-start(f32[2048,512]{0,1:T(8,128)S(1)} %fusion) | copy-start | bytes 12582916
  118.3 5.8 %collective-permute-start = (f32[1024,16]{0,1:T(8,128)S(1)}, f32[1024,16]{0,1:T(8,128)S(1)}, u32[]{:S(2)}, u32[]{:S(2)}) collective-permute-start(f32[1024,16]{0,1:T(8,128)S(1)} %get-tuple-element.7), channel_id=1, source_target_pairs={{0,1},{1,2},{2,3},{3,4},{4,5},{5,6},{6,7},{7,8},{8,9},{9,10},{10,1... | collective-permute-start | bytes 196616 | tf_op jit(solution)/shard_map/ppermute | solution.py:21
  121.9 6.5 %collective-permute-start.1 = (f32[1024,16]{0,1:T(8,128)S(1)}, f32[1024,16]{0,1:T(8,128)S(1)}, u32[]{:S(2)}, u32[]{:S(2)}) collective-permute-start(f32[1024,16]{0,1:T(8,128)S(1)} %get-tuple-element.8), channel_id=1, source_target_pairs={{1,0},{2,1},{3,2},{4,3},{5,4},{6,5},{7,6},{8,7},{9,8},{10,9},{11,1... | collective-permute-start | bytes 196616 | tf_op jit(solution)/shard_map/ppermute | solution.py:23
  128.6 1.4 copy-start.1
